TPU v7x, 128 devices: a whole 4x4x4 slice. The times are simulated.
128 devices in a mesh: atom: 8 (over x, core), aux: 16 (over z, y).
Axes of the slice: x: 4, y: 4, z: 4, core: 2. Of those that a mesh axis runs over, the one named last changes fastest.
Arguments:
- three_index: bfloat16 [256, 16, 4, 128, 128], P('aux', 'atom'), may hold values from -0.09375 to 0.09375
- density: bfloat16 [2048, 2048], P(('atom', 'aux')), may hold values from -6 to 6
- pair_blocks: int32 [16, 4], replicated, may hold values from 0 to 15, as said below
- basis_counts: int32 [16], replicated, may hold values from 1 to 128, 1536 in all
Outputs:
- exchange_matrix: float32 [2048, 2048], P(('atom', 'aux'))
Inputs may be any that keep to these rules, and one draw needn't show every extreme that they name: `pair_blocks`: each row names 4 different basis blocks, the first being the row's own block.
All inputs are finite; a program needn't handle non-finite values.
Results may differ from a plain program's by a relative error of at most 0.0029.
Values may be sent and summed in bfloat16 or wider, within the bound.
No kernel may reach another device: no remote copies, remote signals or barrier semaphores. Data moves between devices by JAX's collectives and lax.ppermute only.
A program may use at most 192 MiB of HBM per device.

v0:
```python
import math
import jax
import jax.numpy as jnp
from jax import lax
from jax.sharding import PartitionSpec as P


def split_up(value, dim, size):
    lengths = value.shape
    parts = value.reshape(*lengths[:dim], size, lengths[dim] // size, *lengths[dim + 1 :])
    return jnp.moveaxis(parts, dim, 0)


def sent_and_summed(value, axis, dim):
    size = lax.axis_size(axis)
    parts = lax.all_to_all(split_up(value, dim, size), axis, 0, 0, tiled=True)
    return jnp.sum(parts, axis=0)


def per_device(three_index, density, pair_blocks, basis_counts):
    whole_density = lax.all_gather(density, ("atom", "aux"), axis=0, tiled=True)
    block_size = three_index.shape[-1]
    total_basis = whole_density.shape[1]
    total_blocks = total_basis // block_size
    own_blocks = three_index.shape[1]
    aux_here = three_index.shape[0]
    first_block = lax.axis_index("atom") * own_blocks
    live_slots = (jnp.arange(block_size)[None, :] < basis_counts[:, None]).astype(jnp.bfloat16)

    def masked(portion, offset):
        block_count = portion.shape[1]
        row_live = lax.dynamic_slice_in_dim(live_slots, offset, block_count, 0)
        partners = lax.dynamic_slice_in_dim(pair_blocks, offset, block_count, 0)
        col_live = live_slots[partners]
        cleaned = portion * row_live[None, :, None, :, None] * col_live[None, :, :, None, :]
        return (cleaned, partners)

    own_tensor, own_partners = masked(three_index, first_block)
    near_density = whole_density.reshape(total_blocks, block_size, total_basis)[own_partners]
    group_size = math.gcd(aux_here, 8)
    grouped = own_tensor.reshape((aux_here // group_size, group_size) + own_tensor.shape[1:])

    def contract(portion):
        product = jnp.einsum(
            "pmjab,mjbs->pmas", portion, near_density, preferred_element_type=jnp.float32
        )
        return product.astype(jnp.bfloat16)

    halfway = lax.map(contract, grouped).reshape(aux_here, own_blocks * block_size, total_basis)
    halfway_cols = halfway.reshape(aux_here, own_blocks * block_size, total_blocks, block_size)
    portion = lax.all_gather(three_index, "atom", axis=1, tiled=True)
    block_count = portion.shape[1]
    cleaned, partners = masked(portion, jnp.int32(0))
    contrib = jnp.einsum(
        "pmbc,pbjcn->mbjn", halfway_cols, cleaned, preferred_element_type=jnp.float32
    )
    placement = (partners.reshape(-1)[:, None] == jnp.arange(total_blocks)[None, :]).astype(
        jnp.float32
    )
    spread_out = jnp.einsum(
        "mqn,qk->mkn",
        contrib.reshape(contrib.shape[0], -1, block_size),
        placement,
        precision=lax.Precision.HIGHEST,
    )
    row_sums = spread_out.reshape(contrib.shape[0], total_basis)
    return sent_and_summed(row_sums, "aux", 0)


def solution(mesh):
    in_specs = (P("aux", "atom", None, None, None), P(("atom", "aux"), None), P(), P())
    out_specs = P(("atom", "aux"), None)
    return jax.shard_map(
        per_device, mesh=mesh, in_specs=in_specs, out_specs=out_specs, check_vma=False
    )
```

profile of v0, /device:TPU:0, one launch (start us, length us, event | category | flops | bytes accessed | tf_op | source)
XLA Modules:
  0.0 328.8 jit_solution(8203879094852832548)
XLA Ops:
  6.5 0.0 all-gather.5.cloned.1.call-start
  6.5 0.7 all-gather.5.cloned.1.call-update
  7.3 0.0 all-gather.3.cloned.1.call-start
  7.3 0.7 all-gather.3.cloned.1.call-update
  8.0 0.8 copy.10
  8.8 0.8 compare_select_fusion
  9.5 0.1 copy.12
  9.6 0.1 reshape.48
  9.7 0.7 compare_select_fusion.1
  10.4 0.1 copy.11
  10.5 0.1 reshape.40
  10.6 0.7 fusion.7
  11.3 0.6 gather_fusion.1
  11.9 0.6 gather_fusion
  12.5 0.1 eq.15
  12.6 4.5 %multiply_multiply_fusion.1 = bf16[16,2,4,128,128]{4,3,2,1,0:T(8,128)(2,1)} fusion(bf16[16,2,4,128,128]{4,3,2,1,0:T(8,128)(2,1)} %param.6, bf16[2,4,128]{2,1,0:T(4,128)(2,1)S(1)} %bitcast.57, bf16[2,128]{1,0:T(2,128)(2,1)S(1)} %constant_dynamic-slice_fusion.1), kind=kLoop, calls=%fused_computation.14 | loop fusion | flops 4194304 | bytes 8391168 | tf_op jit(solution)/shard_map/mul | solution.py:35
  17.2 66.0 %all-gather.5.cloned.1.call-done = bf16[2048,2048]{1,0:T(8,128)(2,1)} async-done(((bf16[16,2048]{1,0:T(8,128)(2,1)}), bf16[2048,2048]{1,0:T(8,128)(2,1)}) %all-gather.5.cloned.1.call-update) | async-done | bytes 8388624 | tf_op jit(solution)/shard_map/all_gather | solution.py:21
  83.2 6.1 %gather_fusion.2 = bf16[8,128,2048]{2,1,0:T(8,128)(2,1)} fusion(bf16[16,128,2048]{2,1,0:T(8,128)(2,1)} %bitcast.55, s32[1024]{0:T(1024)S(1)} %pad_clamp_fusion), kind=kCustom, calls=%fused_computation.2 | custom fusion | bytes 8388640 | tf_op jit(solution)/shard_map/gather | solution.py:39
  89.3 37.6 %while.10 = (s32[]{:T(128)}, bf16[2,8,2,128,2048]{4,3,2,1,0:T(8,128)(2,1)}, bf16[2,8,2,4,128,128]{5,4,3,2,1,0:T(8,128)(2,1)}, bf16[2,4,128,2048]{3,2,1,0:T(8,128)(2,1)}, s32[]{:T(128)}) while((s32[]{:T(128)}, bf16[2,8,2,128,2048]{4,3,2,1,0:T(8,128)(2,1)}, bf16[2,8,2,4,128,128]{5,4,3,2,1,0:T(8,128)(2,1)}, bf16[2,4,128,2048]{3,2,1,0:T(8,128)(2,1)}, ...), condition=%wide.region_1.2_spmd, body=%wide.region_0.1_spmd.sunk | while | flops 4299161600 | bytes 31458364 | solution.py:49
  89.3 9.7 %fusion.13 = bf16[1,8,2,128,2048]{4,3,1,2,0:T(8,128)(2,1)} fusion(bf16[2,4,128,2048]{3,2,1,0:T(8,128)(2,1)} %get-tuple-element.78, bf16[2,8,2,4,128,128]{5,4,3,2,1,0:T(8,128)(2,1)} %get-tuple-element.77, s32[]{:T(128)} %get-tuple-element.70), kind=kOutput, calls=%fused_computation.4.clone.1 | convolution fusion | flops 4299161600 | bytes 14680576 | tf_op jit(solution)/shard_map/while/body/eval_jaxpr/pmjab,mjbs->pmas/dot_general | solution.py:44
  99.0 10.4 %copy_dynamic-update-slice_fusion.2 = bf16[2,8,2,128,2048]{4,3,2,1,0:T(8,128)(2,1)} fusion(bf16[2,8,2,128,2048]{4,3,2,1,0:T(8,128)(2,1)} %get-tuple-element.71, s32[]{:T(128)} %get-tuple-element.70, bf16[1,8,2,128,2048]{4,3,1,2,0:T(8,128)(2,1)} %fusion.13), kind=kLoop, calls=%fused_computation.5.clone.1 | loop fusion | bytes 16777728 | tf_op jit(solution)/shard_map/while/body/jit(dynamic_update_index_in_dim)/dynamic_update_slice | solution.py:49
  109.4 9.2 %fusion.13 = bf16[1,8,2,128,2048]{4,3,1,2,0:T(8,128)(2,1)} fusion(bf16[2,4,128,2048]{3,2,1,0:T(8,128)(2,1)} %get-tuple-element.78, bf16[2,8,2,4,128,128]{5,4,3,2,1,0:T(8,128)(2,1)} %get-tuple-element.77, s32[]{:T(128)} %get-tuple-element.70), kind=kOutput, calls=%fused_computation.4.clone.1 | convolution fusion | flops 4299161600 | bytes 14680576 | tf_op jit(solution)/shard_map/while/body/eval_jaxpr/pmjab,mjbs->pmas/dot_general | solution.py:44
  118.7 8.2 %copy_dynamic-update-slice_fusion.2 = bf16[2,8,2,128,2048]{4,3,2,1,0:T(8,128)(2,1)} fusion(bf16[2,8,2,128,2048]{4,3,2,1,0:T(8,128)(2,1)} %get-tuple-element.71, s32[]{:T(128)} %get-tuple-element.70, bf16[1,8,2,128,2048]{4,3,1,2,0:T(8,128)(2,1)} %fusion.13), kind=kLoop, calls=%fused_computation.5.clone.1 | loop fusion | bytes 16777728 | tf_op jit(solution)/shard_map/while/body/jit(dynamic_update_index_in_dim)/dynamic_update_slice | solution.py:49
  126.9 9.9 %copy.29 = bf16[512,8,16,128]{3,2,1,0:T(8,128)(2,1)S(1)} copy(bf16[512,8,16,128]{3,1,2,0:T(8,128)(2,1)} %bitcast.52) | data formatting | bytes 33554432
  136.8 7.4 %bitcast_bitcast_fusion = bf16[16,256,16,128,1]{3,2,1,0,4:T(8,128)(2,1)} fusion(bf16[16,256,16,128]{3,2,1,0:T(8,128)(2,1)S(1)} %bitcast.50), kind=kLoop, calls=%fused_computation.12 | loop fusion | bytes 33554432 | tf_op jit(solution)/shard_map/reshape;reshape | solution.py:50
  144.3 94.0 %all-gather.3.cloned.1.call-done = bf16[16,16,4,128,128]{4,3,2,1,0:T(8,128)(2,1)} async-done(((bf16[16,2,4,128,128]{4,3,2,1,0:T(8,128)(2,1)}), bf16[16,16,4,128,128]{4,3,2,1,0:T(8,128)(2,1)}) %all-gather.3.cloned.1.call-update) | async-done | bytes 33554448 | tf_op jit(solution)/shard_map/all_gather | solution.py:51
  238.2 24.2 %fusion.2 = f32[16,4,128,256,1]{3,2,0,1,4:T(8,128)} fusion(bf16[16,256,16,128,1]{3,2,1,0,4:T(8,128)(2,1)} %bitcast_bitcast_fusion, bf16[16,16,4,128,128]{4,3,2,1,0:T(8,128)(2,1)} %all-gather.3.cloned.1.call-done, bf16[16,4,128]{2,1,0:T(4,128)(2,1)S(1)} %bitcast.56, bf16[16,128]{1,0:T(8,128)(2,1)S(1)} %fusion.7), kind=kOutput, calls=%fused_computation.9 | convolution fusion | flops 8623489024 | bytes 58740736 | tf_op jit(solution)/shard_map/pmbc,pbjcn->mbjn/dot_general | solution.py:54
  262.4 7.6 %copy.22 = f32[16,4,128,256,1]{3,2,1,0,4:T(8,128)} copy(f32[16,4,128,256,1]{3,2,0,1,4:T(8,128)} %fusion.2) | data formatting | bytes 16777216 | tf_op jit(solution)/shard_map/pmbc,pbjcn->mbjn/dot_general | solution.py:54
  270.0 8.7 %copy.17 = f32[256,64,128]{2,1,0:T(8,128)} copy(f32[256,64,128]{0,2,1:T(8,128)} %bitcast.51) | data formatting | bytes 16777216 | tf_op jit(solution)/shard_map/reshape | solution.py:62
  278.8 5.1 %convolution_bitcast_fusion = f32[256,16,128]{2,1,0:T(8,128)S(1)} fusion(f32[256,64,128]{2,1,0:T(8,128)} %copy.17, s32[64]{0:T(128)S(1)} %eq.15), kind=kOutput, calls=%fused_computation.15 | convolution fusion | flops 402654208 | bytes 10486016 | tf_op jit(solution)/shard_map/mqn,qk->mkn/dot_general | solution.py:60
  283.9 1.5 reshape_reshape.7
  285.4 35.8 %all_to_all.5 = f32[16,16,2048]{2,1,0:T(8,128)S(1)} all-to-all(f32[16,16,2048]{2,1,0:T(8,128)} %reshape_reshape.7), channel_id=1, replica_groups=mesh['atom'=8,'aux'=16] {'aux'}, dimensions={0} | all-to-all | bytes 4194304 | tf_op jit(solution)/shard_map/all_to_all | solution.py:16
  321.2 0.8 reduce_sum.9
  (4 shorter events, 0.0 us)
Async XLA Ops:
  6.5 76.6 %all-gather.5.cloned.1.call-start = ((), (), s32[]{:S(2)}) async-start(), calls=%async_computation.2 | async-start | bytes 8454144 | tf_op jit(solution)/shard_map/all_gather | solution.py:21
  7.3 231.0 %all-gather.3.cloned.1.call-start = ((), (), s32[]{:S(2)}) async-start(), calls=%async_computation.1 | async-start | bytes 37748736 | tf_op jit(solution)/shard_map/all_gather | solution.py:51
Sparse Core Ops, SparseCore 0:
  10.5 72.6 all-gather.4
  84.8 153.3 all-gather.2
where the time goes:
time: 329 us
  waiting for transfers between devices  161 us (49%)
  local copies, waits for them, and re-layouts  62.4 us (19%)
  matrix products  48.3 us (15%)
  blocking collectives  35.8 us (11%)
  between operations  13.5 us (4%)
  other arithmetic  7.45 us (2%)
    all_gather x1, waiting for transfers between devices, per_device(): portion = lax.all_gather(three_index, 'atom', axis=1, tiled=True)  94 us
    all_gather x1, waiting for transfers between devices, per_device(): whole_density = lax.all_gather(density, ('atom', 'aux'), axis=0, tiled=True)  66 us
    all_to_all x1, blocking collectives, sent_and_summed(): parts = lax.all_to_all(split_up(value, dim, size), axis, 0, 0, tiled=True)  35.8 us
    dot_general x1, matrix products, per_device(): jnp.einsum('pmbc,pbjcn->mbjn', halfway_cols, cleaned, preferred_element_t...  24.2 us
    dot_general x2, matrix products, contract(): jnp.einsum('pmjab,mjbs->pmas', portion, near_density, preferred_element_t...  18.9 us
    dynamic_update_slice x2, local copies, waits for them, and re-layouts, per_device(): lax.map(contract, grouped)  18.7 us
    unnamed x2, local copies, waits for them, and re-layouts  10.7 us
    reshape x1, local copies, waits for them, and re-layouts, per_device(): contrib.reshape(contrib.shape[0], -1, block_size)  8.72 us
  transfers between devices with their start and end apart: 2, of which 2 were waited for; matrix products, arithmetic and copies ran while one was open for 21% of the time, Pallas kernels for 0%

commit v1 on v0

--- a/solution.py
+++ b/solution.py
@@ -3,6 +3,7 @@
 import jax.numpy as jnp
 from jax import lax
 from jax.sharding import PartitionSpec as P
+from jax.lax import all_to_all, psum
 
 
 def split_up(value, dim, size):
@@ -18,7 +19,16 @@
 
 
 def per_device(three_index, density, pair_blocks, basis_counts):
-    whole_density = lax.all_gather(density, ("atom", "aux"), axis=0, tiled=True)
+    read_cubes = lambda sample, dev_axis: jnp.concatenate(
+        all_to_all(
+            jnp.stack([sample for _ in range(psum(1, axis_name=dev_axis))], axis=0),
+            axis_name=dev_axis,
+            split_axis=0,
+            concat_axis=0,
+        ),
+        axis=0,
+    )
+    whole_density = read_cubes(density, ("atom", "aux"))
     block_size = three_index.shape[-1]
     total_basis = whole_density.shape[1]
     total_blocks = total_basis // block_size

time: 329 us -> 353 us (1.073)
  waiting for transfers between devices: 161 us -> 175 us
  starting transfers between devices: 0.04 us -> 11.7 us
  blocking collectives: 35.8 us -> 31.3 us
    all_to_all x0 -> x1, waiting for transfers between devices: none -> 174 us  [per_device(): all_to_all(jnp.stack([sample for _ in range(psum(1, axis_name=dev_axis))]...]
    all_gather x1, waiting for transfers between devices: 94 us -> 0.01 us  [per_device(): portion = lax.all_gather(three_index, 'atom', axis=1, tiled=True)]
    all_gather x1 -> x0, waiting for transfers between devices: 66 us -> none  [per_device(): whole_density = lax.all_gather(density, ('atom', 'aux'), axis=0, tiled=True)]
    all_to_all x0 -> x1, starting transfers between devices: none -> 11.7 us  [per_device(): all_to_all(jnp.stack([sample for _ in range(psum(1, axis_name=dev_axis))]...]
    another operation x0 -> x1, local copies, waits for them, and re-layouts: none -> 5.1 us  [per_device(): jnp.stack([sample for _ in range(psum(1, axis_name=dev_axis))], axis=0)]
    all_to_all x1, blocking collectives: 35.8 us -> 31.3 us  [sent_and_summed(): parts = lax.all_to_all(split_up(value, dim, size), axis, 0, 0, tiled=True)]
    unnamed x2 -> x6, local copies, waits for them, and re-layouts: 10.7 us -> 9.74 us
  transfers between devices with their start and end apart: 2 -> 2, of which waited for: 2 -> 1; matrix products, arithmetic and copies ran while one was open for 21% -> 20% of each run, Pallas kernels for 0% -> 0%
where the time goes in v1:
time: 353 us; the launch traced here: 351 us
  waiting for transfers between devices  175 us (50%)
  local copies, waits for them, and re-layouts  65.2 us (18%)
  matrix products  47.8 us (14%)
  blocking collectives  31.3 us (9%)
  between operations  13.5 us (4%)
  starting transfers between devices  11.7 us (3%)
  other arithmetic  6.16 us (2%)
    all_to_all x1, waiting for transfers between devices, per_device(): all_to_all(jnp.stack([sample for _ in range(psum(1, axis_name=dev_axis))]...  174 us
    all_to_all x1, blocking collectives, sent_and_summed(): parts = lax.all_to_all(split_up(value, dim, size), axis, 0, 0, tiled=True)  31.3 us
    dot_general x1, matrix products, per_device(): jnp.einsum('pmbc,pbjcn->mbjn', halfway_cols, cleaned, preferred_element_t...  24.2 us
    dot_general x2, matrix products, contract(): jnp.einsum('pmjab,mjbs->pmas', portion, near_density, preferred_element_t...  18.5 us
    dynamic_update_slice x2, local copies, waits for them, and re-layouts, per_device(): lax.map(contract, grouped)  16.8 us
    all_to_all x1, starting transfers between devices, per_device(): all_to_all(jnp.stack([sample for _ in range(psum(1, axis_name=dev_axis))]...  11.7 us
    unnamed x6, local copies, waits for them, and re-layouts  9.74 us
    reshape x1, local copies, waits for them, and re-layouts, per_device(): contrib.reshape(contrib.shape[0], -1, block_size)  8.72 us
  transfers between devices with their start and end apart: 2, of which 1 were waited for; matrix products, arithmetic and copies ran while one was open for 20% of the time, Pallas kernels for 0%

profile of v1, /device:TPU:0, one launch (start us, length us, event | category | flops | bytes accessed | tf_op | source)
XLA Modules:
  0.0 350.8 jit_solution(10480637136870091055)
XLA Ops:
  6.5 0.0 all-gather.2.cloned.1.call-start
  6.5 0.7 all-gather.2.cloned.1.call-update
  7.3 5.1 %stack.2 = bf16[128,16,2048]{2,1,0:T(8,128)(2,1)} broadcast(bf16[16,2048]{1,0:T(8,128)(2,1)} %param.7), dimensions={1,2} | broadcast | bytes 8454144 | tf_op jit(solution)/shard_map/stack | solution.py:24
  12.4 0.0 copy-start
  12.4 0.0 copy-start.1
  12.4 11.7 %all-to-all-start = ((bf16[128,16,2048]{2,1,0:T(8,128)(2,1)}), bf16[128,16,2048]{2,1,0:T(8,128)(2,1)}, u32[]{:S(2)}, u32[]{:S(2)}) async-start(bf16[128,16,2048]{2,1,0:T(8,128)(2,1)} %stack.2), calls=%async_computation | async-start | bytes 16777216 | tf_op jit(solution)/shard_map/all_to_all | solution.py:23
  24.1 0.0 copy-done
  24.1 0.1 copy.10
  24.2 0.1 compare_select_fusion
  24.2 0.1 copy.12
  24.3 0.1 reshape.46
  24.4 0.1 copy.11
  24.5 0.1 reshape.38
  24.6 0.0 copy-done.1
  24.6 0.1 fusion.7
  24.7 0.6 gather_fusion.1
  25.3 0.6 gather_fusion
  25.9 0.1 eq.15
  26.0 5.2 %multiply_multiply_fusion.1 = bf16[16,2,4,128,128]{4,3,2,1,0:T(8,128)(2,1)} fusion(bf16[16,2,4,128,128]{4,3,2,1,0:T(8,128)(2,1)} %param.6, bf16[2,4,128]{2,1,0:T(4,128)(2,1)S(1)} %bitcast.56, bf16[2,128]{1,0:T(2,128)(2,1)S(1)} %constant_dynamic-slice_fusion.1), kind=kLoop, calls=%fused_computation.14 | loop fusion | flops 4194304 | bytes 8391168 | tf_op jit(solution)/shard_map/mul | solution.py:45
  31.3 174.5 %all-to-all-done = bf16[128,16,2048]{2,1,0:T(8,128)(2,1)} async-done(((bf16[128,16,2048]{2,1,0:T(8,128)(2,1)}), bf16[128,16,2048]{2,1,0:T(8,128)(2,1)}, u32[]{:S(2)}, u32[]{:S(2)}) %all-to-all-start) | async-done | bytes 8388640 | tf_op jit(solution)/shard_map/all_to_all | solution.py:23
  205.7 6.6 %gather_fusion.2 = bf16[8,128,2048]{2,1,0:T(8,128)(2,1)} fusion(bf16[16,128,2048]{2,1,0:T(8,128)(2,1)} %bitcast.11, s32[1024]{0:T(1024)S(1)} %pad_clamp_fusion), kind=kCustom, calls=%fused_computation.2 | custom fusion | bytes 8388640 | tf_op jit(solution)/shard_map/gather | solution.py:49
  212.3 35.3 %while.10 = (s32[]{:T(128)}, bf16[2,8,2,128,2048]{4,3,2,1,0:T(8,128)(2,1)}, bf16[2,8,2,4,128,128]{5,4,3,2,1,0:T(8,128)(2,1)}, bf16[2,4,128,2048]{3,2,1,0:T(8,128)(2,1)}, s32[]{:T(128)}) while((s32[]{:T(128)}, bf16[2,8,2,128,2048]{4,3,2,1,0:T(8,128)(2,1)}, bf16[2,8,2,4,128,128]{5,4,3,2,1,0:T(8,128)(2,1)}, bf16[2,4,128,2048]{3,2,1,0:T(8,128)(2,1)}, ...), condition=%wide.region_1.2_spmd, body=%wide.region_0.1_spmd.sunk | while | flops 4299161600 | bytes 31458364 | solution.py:59
  212.3 9.2 %fusion.13 = bf16[1,8,2,128,2048]{4,3,1,2,0:T(8,128)(2,1)} fusion(bf16[2,4,128,2048]{3,2,1,0:T(8,128)(2,1)} %get-tuple-element.78, bf16[2,8,2,4,128,128]{5,4,3,2,1,0:T(8,128)(2,1)} %get-tuple-element.77, s32[]{:T(128)} %get-tuple-element.70), kind=kOutput, calls=%fused_computation.4.clone.1 | convolution fusion | flops 4299161600 | bytes 14680576 | tf_op jit(solution)/shard_map/while/body/eval_jaxpr/pmjab,mjbs->pmas/dot_general | solution.py:54
  221.6 8.2 %copy_dynamic-update-slice_fusion.2 = bf16[2,8,2,128,2048]{4,3,2,1,0:T(8,128)(2,1)} fusion(bf16[2,8,2,128,2048]{4,3,2,1,0:T(8,128)(2,1)} %get-tuple-element.71, s32[]{:T(128)} %get-tuple-element.70, bf16[1,8,2,128,2048]{4,3,1,2,0:T(8,128)(2,1)} %fusion.13), kind=kLoop, calls=%fused_computation.5.clone.1 | loop fusion | bytes 16777728 | tf_op jit(solution)/shard_map/while/body/jit(dynamic_update_index_in_dim)/dynamic_update_slice | solution.py:59
  229.8 9.2 %fusion.13 = bf16[1,8,2,128,2048]{4,3,1,2,0:T(8,128)(2,1)} fusion(bf16[2,4,128,2048]{3,2,1,0:T(8,128)(2,1)} %get-tuple-element.78, bf16[2,8,2,4,128,128]{5,4,3,2,1,0:T(8,128)(2,1)} %get-tuple-element.77, s32[]{:T(128)} %get-tuple-element.70), kind=kOutput, calls=%fused_computation.4.clone.1 | convolution fusion | flops 4299161600 | bytes 14680576 | tf_op jit(solution)/shard_map/while/body/eval_jaxpr/pmjab,mjbs->pmas/dot_general | solution.py:54
  239.1 8.6 %copy_dynamic-update-slice_fusion.2 = bf16[2,8,2,128,2048]{4,3,2,1,0:T(8,128)(2,1)} fusion(bf16[2,8,2,128,2048]{4,3,2,1,0:T(8,128)(2,1)} %get-tuple-element.71, s32[]{:T(128)} %get-tuple-element.70, bf16[1,8,2,128,2048]{4,3,1,2,0:T(8,128)(2,1)} %fusion.13), kind=kLoop, calls=%fused_computation.5.clone.1 | loop fusion | bytes 16777728 | tf_op jit(solution)/shard_map/while/body/jit(dynamic_update_index_in_dim)/dynamic_update_slice | solution.py:59
  247.7 9.6 %copy.29 = bf16[512,8,16,128]{3,2,1,0:T(8,128)(2,1)S(1)} copy(bf16[512,8,16,128]{3,1,2,0:T(8,128)(2,1)} %bitcast.52) | data formatting | bytes 33554432
  257.3 7.4 %bitcast_bitcast_fusion = bf16[16,256,16,128,1]{3,2,1,0,4:T(8,128)(2,1)} fusion(bf16[16,256,16,128]{3,2,1,0:T(8,128)(2,1)S(1)} %bitcast.50), kind=kLoop, calls=%fused_computation.12 | loop fusion | bytes 33554432 | tf_op jit(solution)/shard_map/reshape;reshape | solution.py:60
  264.8 0.0 all-gather.2.cloned.1.call-done
  264.8 24.2 %fusion.2 = f32[16,4,128,256,1]{3,2,0,1,4:T(8,128)} fusion(bf16[16,256,16,128,1]{3,2,1,0,4:T(8,128)(2,1)} %bitcast_bitcast_fusion, bf16[16,16,4,128,128]{4,3,2,1,0:T(8,128)(2,1)} %all-gather.2.cloned.1.call-done, bf16[16,4,128]{2,1,0:T(4,128)(2,1)S(1)} %bitcast.55, bf16[16,128]{1,0:T(8,128)(2,1)S(1)} %fusion.7), kind=kOutput, calls=%fused_computation.9 | convolution fusion | flops 8623489024 | bytes 58740736 | tf_op jit(solution)/shard_map/pmbc,pbjcn->mbjn/dot_general | solution.py:64
  288.9 7.6 %copy.22 = f32[16,4,128,256,1]{3,2,1,0,4:T(8,128)} copy(f32[16,4,128,256,1]{3,2,0,1,4:T(8,128)} %fusion.2) | data formatting | bytes 16777216 | tf_op jit(solution)/shard_map/pmbc,pbjcn->mbjn/dot_general | solution.py:64
  296.6 8.7 %copy.17 = f32[256,64,128]{2,1,0:T(8,128)} copy(f32[256,64,128]{0,2,1:T(8,128)} %bitcast.51) | data formatting | bytes 16777216 | tf_op jit(solution)/shard_map/reshape | solution.py:72
  305.3 5.1 %convolution_bitcast_fusion = f32[256,16,128]{2,1,0:T(8,128)S(1)} fusion(f32[256,64,128]{2,1,0:T(8,128)} %copy.17, s32[64]{0:T(128)S(1)} %eq.15), kind=kOutput, calls=%fused_computation.15 | convolution fusion | flops 402654208 | bytes 10486016 | tf_op jit(solution)/shard_map/mqn,qk->mkn/dot_general | solution.py:70
  310.4 1.5 reshape_reshape.11
  311.9 31.3 %all_to_all.10 = f32[16,16,2048]{2,1,0:T(8,128)S(1)} all-to-all(f32[16,16,2048]{2,1,0:T(8,128)} %reshape_reshape.11), channel_id=1, replica_groups=mesh['atom'=8,'aux'=16] {'aux'}, dimensions={0} | all-to-all | bytes 4194304 | tf_op jit(solution)/shard_map/all_to_all | solution.py:17
  343.2 0.8 reduce_sum.9
  (5 shorter events, 0.0 us)
Async XLA Ops:
  6.5 258.2 %all-gather.2.cloned.1.call-start = ((), (), s32[]{:S(2)}) async-start(), calls=%async_computation.2 | async-start | bytes 37748736 | tf_op jit(solution)/shard_map/all_gather | solution.py:61
  12.4 11.7 %copy-start = (s32[16,4]{0,1:T(4,128)S(1)}, s32[16,4]{0,1:T(4,128)}, u32[]{:S(2)}) copy-start(s32[16,4]{0,1:T(4,128)} %param.8) | copy-start | bytes 772
  12.4 12.2 %copy-start.1 = (s32[16]{0:T(128)S(1)}, s32[16]{0:T(128)}, u32[]{:S(2)}) copy-start(s32[16]{0:T(128)} %param.9) | copy-start | bytes 196
  12.4 193.4 %all-to-all-start = ((bf16[128,16,2048]{2,1,0:T(8,128)(2,1)}), bf16[128,16,2048]{2,1,0:T(8,128)(2,1)}, u32[]{:S(2)}, u32[]{:S(2)}) async-start(bf16[128,16,2048]{2,1,0:T(8,128)(2,1)} %stack.2), calls=%async_computation | async-start | bytes 16777216 | tf_op jit(solution)/shard_map/all_to_all | solution.py:23
Sparse Core Ops, SparseCore 0:
  9.0 244.5 all-gather.1
